TPU v7x, 256 devices: a whole 4x4x8 slice. The times are simulated.
256 devices in a mesh: dp: 32 (over x, z_lo, y), tensor: 8 (over z_hi, core).
Axes of the slice: x: 4, y: 4, z: 8 (z_hi: 4, z_lo: 2; z = z_hi * 2 + z_lo), core: 2. Of those that a mesh axis runs over, the one named last changes fastest.
Arguments:
- gradient: bfloat16 [2, 2048, 16384], P(None, 'dp', 'tensor'), may hold values from -1000 to 1000
- master: float32 [2, 2048, 16384], P(None, 'dp', 'tensor'), may hold values from -0.046875 to 0.046875
- first_moment: float32 [2, 2048, 16384], P(None, 'dp', 'tensor'), may hold values from -3 to 3
- second_moment: float32 [2, 2048, 16384], P(None, 'dp', 'tensor'), may hold values from 0.05 to 1
- residual: bfloat16 [8192, 16384], P('dp', 'tensor'), may hold values from -1500 to 1500
- norm_gain: float32 [16384], replicated, may hold values from 0.5 to 2
- queries: bfloat16 [8192, 128, 128], P('dp', 'tensor'), may hold values from -170 to 170
- layer_cache: bfloat16 [8192, 2, 8, 32, 128], P('dp', None, 'tensor'), may hold values from -4.5 to 4.5
- fresh_entries: bfloat16 [8192, 2, 8, 128], P('dp', None, 'tensor'), may hold values from -6 to 6
- lengths: int32 [8192], P('dp'), may hold values from 2 to 32, as said below
- shard_table: int32 [32], replicated, may hold values from 0 to 31, each once
Outputs:
- new_first: float32 [2, 2048, 16384], P(None, 'dp', 'tensor')
- new_second: float32 [2, 2048, 16384], P(None, 'dp', 'tensor')
- attended: bfloat16 [8192, 128, 128], P('dp', 'tensor')
- activated: bfloat16 [8192, 2048], P('dp', 'tensor')
Inputs may be any that keep to these rules, and one draw needn't show every extreme that they name: `lengths`: every row has 2 or more valid positions, and in each rollout group's rows one row has all 32. `shard_table`: A permutation of the learner shards.
All inputs are finite; a program needn't handle non-finite values.
Results may differ from a plain program's by a relative error of at most 0.0072.
Values may be sent and summed in bfloat16 or wider, within the bound.
A program may use at most 128 MiB of HBM per device.

v0:
```python
import math

import jax
import jax.numpy as jnp
from jax import lax
from jax.sharding import PartitionSpec as P

LEARN_RATE = 0.001
CLIP_LEVEL = 0.5
CLIP_EPSILON = 1e-06
FIRST_DECAY = 0.9
SECOND_DECAY = 0.95
FIRST_CORRECTION = 1.0 - 0.9**10
SECOND_CORRECTION = 1.0 - 0.95**10
ADAM_EPSILON = 1e-08
NORM_EPSILON = 1e-05


def adam_update(gradient, master, first_moment, second_moment):
    entry_count = (
        gradient.shape[0]
        * gradient.shape[1]
        * lax.axis_size("dp")
        * gradient.shape[2]
        * lax.axis_size("tensor")
    )
    gradient_wide = gradient.astype(jnp.float32)
    local_sum = jnp.sum(gradient_wide * gradient_wide)
    total_sum = lax.psum(local_sum, ("dp", "tensor"))
    clip_limit = CLIP_LEVEL * math.sqrt(entry_count)
    clip_factor = jnp.minimum(1.0, clip_limit / (jnp.sqrt(total_sum) + CLIP_EPSILON))
    clipped = gradient_wide * clip_factor
    new_first = FIRST_DECAY * first_moment + (1.0 - FIRST_DECAY) * clipped
    new_second = SECOND_DECAY * second_moment + (1.0 - SECOND_DECAY) * clipped * clipped
    adam_step = (
        new_first / FIRST_CORRECTION / (jnp.sqrt(new_second / SECOND_CORRECTION) + ADAM_EPSILON)
    )
    fresh_weight = (master - LEARN_RATE * adam_step).astype(jnp.bfloat16)
    return (new_first, new_second, fresh_weight)


def attend(queries, layer_cache, fresh_entries, lengths):
    row_count, head_count, head_width = queries.shape
    group_count = layer_cache.shape[2]
    per_group = head_count // group_count
    score_scale = 1.0 / math.sqrt(head_width)
    grouped = queries.reshape(row_count, group_count, per_group, head_width)
    cached_keys = layer_cache[:, 0]
    cached_values = layer_cache[:, 1]
    scores = (
        jnp.einsum("rghd,rgpd->rghp", grouped, cached_keys, preferred_element_type=jnp.float32)
        * score_scale
    )
    own_score = (
        jnp.einsum(
            "rghd,rgd->rgh", grouped, fresh_entries[:, 0], preferred_element_type=jnp.float32
        )
        * score_scale
    )
    positions = lax.broadcasted_iota(jnp.int32, (row_count, 1, 1, cached_keys.shape[2]), 3)
    in_range = positions < lengths[:, None, None, None]
    scores = jnp.where(in_range, scores, -jnp.inf)
    row_peak = jnp.maximum(jnp.max(scores, axis=3), own_score)
    cached_exp = jnp.exp(scores - row_peak[..., None])
    own_exp = jnp.exp(own_score - row_peak)
    denominator = jnp.sum(cached_exp, axis=3) + own_exp
    cached_prob = (cached_exp / denominator[..., None]).astype(jnp.bfloat16)
    own_prob = (own_exp / denominator).astype(jnp.bfloat16)
    combined = jnp.einsum(
        "rghp,rgpd->rghd", cached_prob, cached_values, preferred_element_type=jnp.float32
    )
    combined = (
        combined
        + own_prob[..., None].astype(jnp.float32)
        * fresh_entries[:, 1].astype(jnp.float32)[:, :, None, :]
    )
    return combined.reshape(row_count, head_count, head_width).astype(jnp.bfloat16)


def per_device(
    gradient,
    master,
    first_moment,
    second_moment,
    residual,
    norm_gain,
    queries,
    layer_cache,
    fresh_entries,
    lengths,
    shard_table,
):
    new_first, new_second, fresh_weight = adam_update(gradient, master, first_moment, second_moment)
    row_count = residual.shape[0]
    shard_count = lax.axis_size("dp")
    rank_count = lax.axis_size("tensor")
    unit_block = fresh_weight.shape[1] // rank_count
    gathered = lax.all_gather(residual, "tensor", axis=1, tiled=True)
    gathered_wide = gathered.astype(jnp.float32)
    mean_square = jnp.mean(gathered_wide * gathered_wide, axis=1, keepdims=True)
    normed = (gathered_wide * lax.rsqrt(mean_square + NORM_EPSILON) * norm_gain).astype(
        jnp.bfloat16
    )
    regrouped = lax.all_to_all(fresh_weight, "tensor", split_axis=1, concat_axis=2, tiled=True)
    projected = jnp.einsum(
        "xk,cuk->xcu",
        normed,
        lax.all_gather(regrouped, "dp", axis=1, tiled=True),
        preferred_element_type=jnp.float32,
    )
    projected = projected.reshape(row_count, 2, shard_count, unit_block)
    hidden = jax.nn.silu(projected[:, 0]) * projected[:, 1]
    ordered = jnp.take(hidden, shard_table, axis=1)
    activated = ordered.reshape(row_count, shard_count * unit_block).astype(jnp.bfloat16)
    attended = attend(queries, layer_cache, fresh_entries, lengths)
    return (new_first, new_second, attended, activated)


def solution(mesh):
    return jax.shard_map(
        per_device,
        mesh=mesh,
        in_specs=(
            P(None, "dp", "tensor"),
            P(None, "dp", "tensor"),
            P(None, "dp", "tensor"),
            P(None, "dp", "tensor"),
            P("dp", "tensor"),
            P(),
            P("dp", "tensor", None),
            P("dp", None, "tensor", None, None),
            P("dp", None, "tensor", None),
            P("dp"),
            P(),
        ),
        out_specs=(
            P(None, "dp", "tensor"),
            P(None, "dp", "tensor"),
            P("dp", "tensor", None),
            P("dp", "tensor"),
        ),
        check_vma=False,
    )
```

profile of v0, /device:TPU:1, one launch (start us, length us, event | category | flops | bytes accessed | tf_op | source)
XLA Modules:
  0.0 351.8 jit_solution(8791076577248445641)
XLA Ops:
  7.2 0.7 all-gather.3.cloned.1.call-update
  7.9 0.0 all-gather.5.cloned.1.call-start
  8.0 1.9 fusion.23
  9.9 97.1 %psum.7 = f32[]{:T(128)} all-reduce(f32[]{:T(128)} %fusion.23), channel_id=1, replica_groups=mesh['dp'=32,'tensor'=8] {'dp','tensor'}, use_global_device_ids=true, to_apply=%region_1.0 | all-reduce | flops 1 | bytes 8 | tf_op jit(solution)/shard_map/psum | solution.py:29
  107.7 3.8 %subtract_convert_fusion = (bf16[2,64,2048]{2,1,0:T(8,128)(2,1)S(1)}, f32[2,64,2048]{2,1,0:T(8,128)}, f32[2,64,2048]{2,1,0:T(8,128)}) fusion(f32[2,64,2048]{2,1,0:T(8,128)S(1)} %copy-done.1, f32[]{:T(128)S(6)} %min_shard_map.3, bf16[2,64,2048]{2,1,0:T(8,128)(2,1)} %param.11, f32[2,64,2048]{2,1,0:T(8,128)} %param.14, f32[2,64,2048]{2,1,0:T(8,128)} %param.13), kind=kLoop, calls=%fused_computation.30 | loop fusion | flops 4194304 | bytes 6291460 | tf_op jit(solution)/shard_map/convert_element_type | solution.py:38
  111.5 0.5 copy.36
  112.1 19.4 %all_to_all.18 = bf16[2,64,2048]{2,0,1:T(2,128)(2,1)S(1)} all-to-all(bf16[2,64,2048]{2,0,1:T(2,128)(2,1)S(1)} %copy.36), channel_id=1, replica_groups=mesh['dp'=32,'tensor'=8] {'tensor'}, dimensions={1} | all-to-all | bytes 1048576 | tf_op jit(solution)/shard_map/all_to_all | solution.py:104
  131.5 1.0 copy.37
  132.5 0.2 fusion.40
  132.7 0.1 broadcast_in_dim.37
  132.8 0.1 broadcast_in_dim.38
  132.9 0.1 iota_compare_fusion
  133.1 0.7 fusion.32
  133.7 3.1 fusion.14
  136.8 1.3 fusion.15
  138.1 0.1 fusion.35
  138.2 3.7 %add_convert_fusion = bf16[256,16,128]{2,1,0:T(8,128)(2,1)} fusion(bf16[256,2,1,32,128]{4,3,2,1,0:T(8,128)(2,1)S(1)} %copy-done.2, f32[256,16,32]{2,1,0:T(8,128)S(1)} %get-tuple-element.24, f32[256,128]{1,0:T(8,128)S(1)} %bitcast.54, f32[256,16]{1,0:T(8,128)S(1)} %get-tuple-element.20, f32[256,16]{1,0:T(8,128)S(1)} %get-tuple-element.19, ...), kind=kOutput, calls=%fused_computation.14 | convolution fusion | flops 35782656 | bytes 5799936 | tf_op jit(solution)/shard_map/rghp,rgpd->rghd/dot_general | solution.py:69
  141.9 5.2 %fusion = f32[256]{0:T(256)S(1)} fusion(bf16[256,16384]{1,0:T(8,128)(2,1)} %all-gather.3.cloned.1.call-done), kind=kLoop, calls=%fused_computation.3 | loop fusion | flops 12582656 | bytes 8389632 | tf_op jit(solution)/shard_map/reduce_sum | solution.py:100
  147.1 184.3 %all-gather.5.cloned.1.call-done = bf16[2,256,16384]{2,1,0:T(8,128)(2,1)} async-done(((bf16[2,8,16384]{2,1,0:T(8,128)(2,1)}), bf16[2,256,16384]{2,1,0:T(8,128)(2,1)}) %all-gather.5.cloned.1.call-update) | async-done | bytes 16777232 | tf_op jit(solution)/shard_map/all_gather | solution.py:108
  331.4 12.0 %fusion.19 = f32[256,2,32,8]{0,3,2,1:T(8,128)S(1)} fusion(bf16[2,256,16384]{2,1,0:T(8,128)(2,1)} %all-gather.5.cloned.1.call-done, bf16[256,16384]{1,0:T(8,128)(2,1)} %all-gather.3.cloned.1.call-done, f32[16384]{0:T(1024)S(1)} %copy-done.5, f32[256]{0:T(256)S(1)} %add_rsqrt_fusion), kind=kOutput, calls=%fused_computation.26 | convolution fusion | flops 4311744512 | bytes 25756672 | tf_op jit(solution)/shard_map/xk,cuk->xcu/dot_general | solution.py:105
  343.4 0.1 fusion.30
  343.5 0.6 gather_fusion
  344.1 0.1 fusion.31
  344.2 0.8 copy.38
  (23 shorter events, 0.1 us)
Async XLA Ops:
  7.2 125.9 %copy-start = (bf16[256,16,128]{2,1,0:T(8,128)(2,1)S(1)}, bf16[256,16,128]{2,1,0:T(8,128)(2,1)}, u32[]{:S(2)}) copy-start(bf16[256,16,128]{2,1,0:T(8,128)(2,1)} %param.17) | copy-start | bytes 3145732
  7.2 100.5 %copy-start.1 = (f32[2,64,2048]{2,1,0:T(8,128)S(1)}, f32[2,64,2048]{2,1,0:T(8,128)}, u32[]{:S(2)}) copy-start(f32[2,64,2048]{2,1,0:T(8,128)} %param.12) | copy-start | bytes 3145732
  7.2 134.7 %all-gather.3.cloned.1.call-start = ((), (), s32[]{:S(2)}) async-start(), calls=%async_computation.1 | async-start | bytes 9437184 | tf_op jit(solution)/shard_map/all_gather | solution.py:98
  7.9 323.5 %all-gather.5.cloned.1.call-start = ((), (), s32[]{:S(2)}) async-start(), calls=%async_computation.2 | async-start | bytes 17301504 | tf_op jit(solution)/shard_map/all_gather | solution.py:108
  111.5 20.9 %copy-start.3 = (bf16[256,2,1,128]{3,1,2,0:T(2,128)(2,1)S(1)}, bf16[256,2,1,128]{3,1,2,0:T(2,128)(2,1)}, u32[]{:S(2)}) copy-start(bf16[256,2,1,128]{3,1,2,0:T(2,128)(2,1)} %param.19) | copy-start | bytes 393220
  111.5 21.2 %copy-start.6 = (s32[32]{0:T(128)S(1)}, s32[32]{0:T(128)}, u32[]{:S(2)}) copy-start(s32[32]{0:T(128)} %param.21) | copy-start | bytes 388
  111.5 21.4 %copy-start.4 = (s32[256]{0:T(256)S(1)}, s32[256]{0:T(256)}, u32[]{:S(2)}) copy-start(s32[256]{0:T(256)} %param.20) | copy-start | bytes 3076
  133.7 4.5 %copy-start.2 = (bf16[256,2,1,32,128]{4,3,2,1,0:T(8,128)(2,1)S(1)}, bf16[256,2,1,32,128]{4,3,2,1,0:T(8,128)(2,1)}, u32[]{:S(2)}) copy-start(bf16[256,2,1,32,128]{4,3,2,1,0:T(8,128)(2,1)} %param.18) | copy-start | bytes 12582916
  141.9 189.5 %copy-start.5 = (f32[16384]{0:T(1024)S(1)}, f32[16384]{0:T(1024)}, u32[]{:S(2)}) copy-start(f32[16384]{0:T(1024)} %param.16) | copy-start | bytes 196612
Sparse Core Ops, SparseCore 0:
  9.8 82.1 all-gather.2
  132.6 198.7 all-gather.4
where the time goes:
time: 352 us
  waiting for transfers between devices  185 us (53%)
  blocking collectives  116 us (33%)
  matrix products  19.5 us (6%)
  between operations  15 us (4%)
  other arithmetic  12.8 us (4%)
    all_gather x1, waiting for transfers between devices, per_device(): lax.all_gather(regrouped, 'dp', axis=1, tiled=True)  184 us
    psum x1, blocking collectives, adam_update(): total_sum = lax.psum(local_sum, ('dp', 'tensor'))  97.1 us
    all_to_all x1, blocking collectives, per_device(): lax.all_to_all(fresh_weight, 'tensor', split_axis=1, concat_axis=2, tiled...  19.4 us
    dot_general x1, matrix products, per_device(): jnp.einsum('xk,cuk->xcu', normed, lax.all_gather(regrouped, 'dp', axis=1,...  12 us
  transfers between devices with their start and end apart: 2, of which 1 were waited for; matrix products, arithmetic and copies ran while one was open for 6% of the time, Pallas kernels for 0%

commit v1 on v0

--- a/solution.py
+++ b/solution.py
@@ -14,22 +14,13 @@
 SECOND_CORRECTION = 1.0 - 0.95**10
 ADAM_EPSILON = 1e-08
 NORM_EPSILON = 1e-05
+LINE = 4
 
 
-def adam_update(gradient, master, first_moment, second_moment):
-    entry_count = (
-        gradient.shape[0]
-        * gradient.shape[1]
-        * lax.axis_size("dp")
-        * gradient.shape[2]
-        * lax.axis_size("tensor")
-    )
-    gradient_wide = gradient.astype(jnp.float32)
-    local_sum = jnp.sum(gradient_wide * gradient_wide)
-    total_sum = lax.psum(local_sum, ("dp", "tensor"))
+def adam_update(gradient, master, first_moment, second_moment, total_sum, entry_count):
     clip_limit = CLIP_LEVEL * math.sqrt(entry_count)
     clip_factor = jnp.minimum(1.0, clip_limit / (jnp.sqrt(total_sum) + CLIP_EPSILON))
-    clipped = gradient_wide * clip_factor
+    clipped = gradient.astype(jnp.float32) * clip_factor
     new_first = FIRST_DECAY * first_moment + (1.0 - FIRST_DECAY) * clipped
     new_second = SECOND_DECAY * second_moment + (1.0 - SECOND_DECAY) * clipped * clipped
     adam_step = (
@@ -90,28 +81,49 @@
     lengths,
     shard_table,
 ):
-    new_first, new_second, fresh_weight = adam_update(gradient, master, first_moment, second_moment)
-    row_count = residual.shape[0]
-    shard_count = lax.axis_size("dp")
-    rank_count = lax.axis_size("tensor")
-    unit_block = fresh_weight.shape[1] // rank_count
-    gathered = lax.all_gather(residual, "tensor", axis=1, tiled=True)
-    gathered_wide = gathered.astype(jnp.float32)
-    mean_square = jnp.mean(gathered_wide * gathered_wide, axis=1, keepdims=True)
-    normed = (gathered_wide * lax.rsqrt(mean_square + NORM_EPSILON) * norm_gain).astype(
-        jnp.bfloat16
+    rows, width = residual.shape
+    shards = lax.axis_size("dp")
+    ranks = lax.axis_size("tensor")
+    near = [[g * LINE + y for y in range(LINE)] for g in range(shards // LINE)]
+    far = [[g * LINE + y for g in range(shards // LINE)] for y in range(LINE)]
+    planes = shards // LINE
+
+    wide = residual.astype(jnp.float32)
+    row_sum = jnp.sum(wide * wide, axis=1)
+    gradient_wide = gradient.astype(jnp.float32)
+    grad_sum = jnp.sum(gradient_wide * gradient_wide)
+    sums = lax.psum(jnp.concatenate([row_sum, jnp.broadcast_to(grad_sum, (rows,))]), "tensor")
+    total_sum = lax.psum(sums[rows], "dp")
+    row_sum, total_sum = lax.optimization_barrier((sums[:rows], total_sum))
+
+    me = lax.axis_index("tensor")
+    gain = lax.dynamic_slice_in_dim(norm_gain, me * width, width)
+    scale = lax.rsqrt(row_sum / (width * ranks) + NORM_EPSILON)
+    normed = (wide * scale[:, None] * gain).astype(jnp.bfloat16)
+    normed = lax.all_gather(normed, "dp", axis=0, tiled=True, axis_index_groups=near)
+
+    new_first, new_second, fresh_weight = adam_update(
+        gradient, master, first_moment, second_moment, total_sum, gradient.size * shards * ranks
     )
-    regrouped = lax.all_to_all(fresh_weight, "tensor", split_axis=1, concat_axis=2, tiled=True)
-    projected = jnp.einsum(
-        "xk,cuk->xcu",
-        normed,
-        lax.all_gather(regrouped, "dp", axis=1, tiled=True),
-        preferred_element_type=jnp.float32,
+    units = fresh_weight.shape[1] // ranks
+    weights = lax.all_gather(fresh_weight, "dp", axis=0, axis_index_groups=far)
+    flat = weights.reshape(planes * 2 * ranks * units, width)
+    partial = lax.dot_general(
+        flat, normed, (((1,), (1,)), ((), ())), preferred_element_type=jnp.float32
+    ).astype(jnp.bfloat16)
+    partial = partial.reshape(planes, 2, ranks, units, LINE * rows).transpose(2, 0, 1, 3, 4)
+    partial = partial.reshape(ranks, planes * 2 * units, LINE * rows)
+    summed = lax.psum_scatter(partial, "tensor", scatter_dimension=0, tiled=False)
+    summed = summed.astype(jnp.float32).reshape(planes, 2, units, LINE * rows)
+    hidden = (jax.nn.silu(summed[:, 0]) * summed[:, 1]).astype(jnp.bfloat16)
+    hidden = hidden.reshape(planes * units, LINE * rows)
+    hidden = lax.all_to_all(
+        hidden, "dp", split_axis=1, concat_axis=0, tiled=True, axis_index_groups=near
     )
-    projected = projected.reshape(row_count, 2, shard_count, unit_block)
-    hidden = jax.nn.silu(projected[:, 0]) * projected[:, 1]
-    ordered = jnp.take(hidden, shard_table, axis=1)
-    activated = ordered.reshape(row_count, shard_count * unit_block).astype(jnp.bfloat16)
+    hidden = hidden.reshape(LINE, planes, units, rows).transpose(1, 0, 2, 3)
+    hidden = hidden.reshape(shards, units, rows)
+    ordered = jnp.take(hidden, shard_table, axis=0)
+    activated = ordered.reshape(shards * units, rows).T
     attended = attend(queries, layer_cache, fresh_entries, lengths)
     return (new_first, new_second, attended, activated)
 

time: 352 us -> 330 us (0.938)
  blocking collectives: 116 us -> 86.9 us
  starting transfers between devices: 0.08 us -> 4.6 us
  matrix products: 19.5 us -> 15.4 us
  local copies, waits for them, and re-layouts: 3.1 us -> 6.76 us
    all_gather x2, waiting for transfers between devices: 184 us -> 150 us  [the longest x1 95.2 us: per_device(): weights = lax.all_gather(fresh_weight, 'dp', axis=0, axis_index_groups=far)]
    reduce_scatter x0 -> x1, waiting for transfers between devices: none -> 32.4 us  [per_device(): lax.psum_scatter(partial, 'tensor', scatter_dimension=0, tiled=False)]
    all_to_all x1 -> x0, blocking collectives: 19.4 us -> none  [per_device(): lax.all_to_all(fresh_weight, 'tensor', split_axis=1, concat_axis=2, tiled...]
    psum x1 -> x2, blocking collectives: 97.1 us -> 86.9 us  [the longest x1 69.3 us: per_device(): total_sum = lax.psum(sums[rows], 'dp')]
    all_to_all x0 -> x1, waiting for transfers between devices: none -> 4.82 us  [per_device(): lax.all_to_all(hidden, 'dp', split_axis=1, concat_axis=0, tiled=True, axi...]
    all_to_all x0 -> x1, starting transfers between devices: none -> 4.47 us  [per_device(): lax.all_to_all(hidden, 'dp', split_axis=1, concat_axis=0, tiled=True, axi...]
    dot_general x1, matrix products: 12 us -> 7.99 us  [per_device(): lax.dot_general(flat, normed, (((1,), (1,)), ((), ())), preferred_element...]
  transfers between devices with their start and end apart: 2 -> 4, of which waited for: 1 -> 4; matrix products, arithmetic and copies ran while one was open for 6% -> 4% of each run, Pallas kernels for 0% -> 0%
where the time goes in v1:
time: 330 us; the launch traced here: 328 us
  waiting for transfers between devices  188 us (57%)
  blocking collectives  86.9 us (26%)
  matrix products  15.4 us (5%)
  between operations  14.7 us (4%)
  other arithmetic  11.7 us (4%)
  local copies, waits for them, and re-layouts  6.76 us (2%)
  starting transfers between devices  4.6 us (1%)
    all_gather x1, waiting for transfers between devices, per_device(): weights = lax.all_gather(fresh_weight, 'dp', axis=0, axis_index_groups=far)  95.2 us
    psum x1, blocking collectives, per_device(): total_sum = lax.psum(sums[rows], 'dp')  69.3 us
    all_gather x1, waiting for transfers between devices, per_device(): lax.all_gather(normed, 'dp', axis=0, tiled=True, axis_index_groups=near)  55.1 us
    reduce_scatter x1, waiting for transfers between devices, per_device(): lax.psum_scatter(partial, 'tensor', scatter_dimension=0, tiled=False)  32.4 us
    psum x1, blocking collectives, per_device(): lax.psum(jnp.concatenate([row_sum, jnp.broadcast_to(grad_sum, (rows,))]),...  17.6 us
    dot_general x1, matrix products, per_device(): lax.dot_general(flat, normed, (((1,), (1,)), ((), ())), preferred_element...  7.99 us
  transfers between devices with their start and end apart: 4, of which 4 were waited for; matrix products, arithmetic and copies ran while one was open for 4% of the time, Pallas kernels for 0%

profile of v1, /device:TPU:1, one launch (start us, length us, event | category | flops | bytes accessed | tf_op | source)
XLA Modules:
  0.0 327.7 jit_solution(12909941378476952959)
XLA Ops:
  7.2 1.6 fusion
  8.9 2.0 fusion.15
  10.9 0.6 concatenate.3
  11.5 17.6 %psum.14 = f32[512]{0:T(512)S(1)} all-reduce(f32[512]{0:T(512)S(1)} %concatenate.3), channel_id=1, replica_groups=mesh['dp'=32,'tensor'=8] {'tensor'}, use_global_device_ids=true, to_apply=%region_2.0 | all-reduce | flops 512 | bytes 4096 | tf_op jit(solution)/shard_map/psum | solution.py:95
  29.7 69.3 %psum.15 = f32[]{:T(128)} all-reduce(f32[]{:T(128)} %bitcast), channel_id=1, replica_groups=mesh['dp'=32,'tensor'=8] {'dp'}, use_global_device_ids=true, to_apply=%region_3.0 | all-reduce | flops 1 | bytes 8 | tf_op jit(solution)/shard_map/psum | solution.py:96
  99.0 0.7 dynamic_slice.3
  99.7 1.3 fusion.2
  101.8 3.9 %subtract_convert_fusion = (bf16[2,64,2048]{2,1,0:T(8,128)(2,1)}, f32[2,64,2048]{2,1,0:T(8,128)}, f32[2,64,2048]{2,1,0:T(8,128)}) fusion(f32[2,64,2048]{2,1,0:T(8,128)} %param.12, f32[]{:T(128)S(6)} %min_shard_map.3, bf16[2,64,2048]{2,1,0:T(8,128)(2,1)S(1)} %copy-done.2, f32[2,64,2048]{2,1,0:T(8,128)} %param.14, f32[2,64,2048]{2,1,0:T(8,128)} %param.13), kind=kLoop, calls=%fused_computation.26 | loop fusion | flops 4194304 | bytes 6291460 | tf_op jit(solution)/shard_map/convert_element_type | solution.py:29
  105.8 55.1 %all-gather.4.cloned.1.call-done = bf16[1024,2048]{1,0:T(8,128)(2,1)} async-done(((bf16[256,2048]{1,0:T(8,128)(2,1)}), bf16[1024,2048]{1,0:T(8,128)(2,1)}) %all-gather.4.cloned.1.call-update) | async-done | bytes 4194320 | tf_op jit(solution)/shard_map/all_gather | solution.py:103
  160.8 95.2 %all-gather.6.cloned.1.call-done = bf16[16,64,2048]{2,1,0:T(8,128)(2,1)} async-done(((bf16[2,64,2048]{2,1,0:T(8,128)(2,1)}), bf16[16,64,2048]{2,1,0:T(8,128)(2,1)}) %all-gather.6.cloned.1.call-update) | async-done | bytes 4194320 | tf_op jit(solution)/shard_map/all_gather | solution.py:109
  256.1 8.0 %convolution_convert_fusion = bf16[1024,1024]{1,0:T(8,128)(2,1)S(1)} fusion(bf16[1024,2048]{1,0:T(8,128)(2,1)} %bitcast.67, bf16[1024,2048]{1,0:T(8,128)(2,1)} %all-gather.4.cloned.1.call-done), kind=kOutput, calls=%fused_computation.16 | convolution fusion | flops 4296015872 | bytes 10485760 | tf_op jit(solution)/shard_map/dot_general | solution.py:111
  264.0 1.5 copy.40
  265.6 0.9 copy-done.4
  267.0 0.6 fusion.25
  267.7 3.1 fusion.9
  270.8 1.3 fusion.10
  272.1 3.7 %add_convert_fusion = bf16[256,16,128]{2,1,0:T(8,128)(2,1)} fusion(bf16[256,2,1,32,128]{4,3,2,1,0:T(8,128)(2,1)S(1)} %copy-done.3, f32[256,16,32]{2,1,0:T(8,128)S(1)} %get-tuple-element.34, f32[256,128]{1,0:T(8,128)S(1)} %bitcast.65, f32[256,16]{1,0:T(8,128)S(1)} %get-tuple-element.30, f32[256,16]{1,0:T(8,128)S(1)} %get-tuple-element.29, ...), kind=kOutput, calls=%fused_computation.10 | convolution fusion | flops 35782656 | bytes 5799936 | tf_op jit(solution)/shard_map/rghp,rgpd->rghd/dot_general | solution.py:60
  275.9 32.4 %reduce-scatter.2.cloned.1.call-done = bf16[1,128,1024]{2,1,0:T(8,128)(2,1)} async-done(((bf16[8,128,1024]{2,1,0:T(8,128)(2,1)}), bf16[1,128,1024]{2,1,0:T(8,128)(2,1)}) %reduce-scatter.2.cloned.1.call-update) | async-done | bytes 262160 | tf_op jit(solution)/shard_map/reduce_scatter | solution.py:116
  308.3 1.0 convert.2
  309.8 0.7 copy.43
  310.4 4.5 %all-to-all-start = ((bf16[64,4,256]{2,0,1:T(8,128)(2,1)}), bf16[64,4,256]{2,0,1:T(8,128)(2,1)S(1)}, u32[]{:S(2)}, u32[]{:S(2)}) async-start(bf16[64,4,256]{2,0,1:T(8,128)(2,1)} %copy.43), calls=%async_computation.1 | async-start | bytes 262144 | tf_op jit(solution)/shard_map/all_to_all | solution.py:120
  314.9 4.8 %all-to-all-done = bf16[64,4,256]{2,0,1:T(8,128)(2,1)S(1)} async-done(((bf16[64,4,256]{2,0,1:T(8,128)(2,1)}), bf16[64,4,256]{2,0,1:T(8,128)(2,1)S(1)}, u32[]{:S(2)}, u32[]{:S(2)}) %all-to-all-start) | async-done | bytes 131104 | tf_op jit(solution)/shard_map/all_to_all | solution.py:120
  319.7 0.6 gather_fusion
  320.4 0.8 copy.45
  (38 shorter events, 1.8 us)
Async XLA Ops:
  7.2 259.8 %copy-start = (bf16[256,16,128]{2,1,0:T(8,128)(2,1)S(1)}, bf16[256,16,128]{2,1,0:T(8,128)(2,1)}, u32[]{:S(2)}) copy-start(bf16[256,16,128]{2,1,0:T(8,128)(2,1)} %param.17) | copy-start | bytes 3145732
  7.2 92.5 %copy-start.1 = (bf16[256,2048]{1,0:T(8,128)(2,1)S(1)}, bf16[256,2048]{1,0:T(8,128)(2,1)}, u32[]{:S(2)}) copy-start(bf16[256,2048]{1,0:T(8,128)(2,1)} %param.15) | copy-start | bytes 3145732
  7.2 153.7 %all-gather.4.cloned.1.call-start = ((), (), s32[]{:S(2)}) async-start(), calls=%async_computation.2 | async-start | bytes 5242880 | tf_op jit(solution)/shard_map/all_gather | solution.py:103
  8.9 92.9 %copy-start.2 = (bf16[2,64,2048]{2,1,0:T(8,128)(2,1)S(1)}, bf16[2,64,2048]{2,1,0:T(8,128)(2,1)}, u32[]{:S(2)}) copy-start(bf16[2,64,2048]{2,1,0:T(8,128)(2,1)} %param.11) | copy-start | bytes 1572868
  101.0 155.0 %all-gather.6.cloned.1.call-start = ((), (), s32[]{:S(2)}) async-start(), calls=%async_computation.4 | async-start | bytes 4718592 | tf_op jit(solution)/shard_map/all_gather | solution.py:109
  105.7 202.6 %reduce-scatter.2.cloned.1.call-start = ((), (), s32[]{:S(2)}) async-start(), calls=%async_computation.3 | async-start | bytes 2359296 | tf_op jit(solution)/shard_map/reduce_scatter | solution.py:116
  265.6 0.9 copy-start.4
  265.6 1.1 copy-start.6
  265.6 1.3 copy-start.5
  267.7 4.5 %copy-start.3 = (bf16[256,2,1,32,128]{4,3,2,1,0:T(8,128)(2,1)S(1)}, bf16[256,2,1,32,128]{4,3,2,1,0:T(8,128)(2,1)}, u32[]{:S(2)}) copy-start(bf16[256,2,1,32,128]{4,3,2,1,0:T(8,128)(2,1)} %param.18) | copy-start | bytes 12582916
  310.4 9.3 %all-to-all-start = ((bf16[64,4,256]{2,0,1:T(8,128)(2,1)}), bf16[64,4,256]{2,0,1:T(8,128)(2,1)S(1)}, u32[]{:S(2)}, u32[]{:S(2)}) async-start(bf16[64,4,256]{2,0,1:T(8,128)(2,1)} %copy.43), calls=%async_computation.1 | async-start | bytes 262144 | tf_op jit(solution)/shard_map/all_to_all | solution.py:120
Sparse Core Ops, SparseCore 0:
  101.1 59.6 all-gather.3
  162.6 93.3 all-gather.5
  265.7 42.5 reduce-scatter.1
